TPU v7x, 256 devices: a whole 4x4x8 slice. The times are simulated.
256 devices in a mesh: tm: 32 (over y, z), mp: 8 (over x, core).
Axes of the slice: x: 4, y: 4, z: 8, core: 2. Of those that a mesh axis runs over, the one named last changes fastest.
Arguments:
- frames_in: bfloat16 [16384, 1024], P('tm'), may hold values from -16 to 16
- queries: bfloat16 [16384, 1024], P('tm', 'mp'), may hold values from -6 to 6
- keys: bfloat16 [16384, 1024], P('tm', 'mp'), may hold values from -6 to 6
- values: bfloat16 [16384, 1024], P('tm', 'mp'), may hold values from -6 to 6
- segment_edges: int32 [2, 16384], P(None, 'tm'), may hold values from 0 to 16383, as said below
- out_proj: bfloat16 [1024, 1024], P('mp'), may hold values from -0.1875 to 0.1875
- expert_ids: int32 [16384, 2], P('tm'), may hold values from 0 to 63, all different within a row; in each aligned block of 512 rows (0 to 511, 512 to 1023, ...) at most 32 rows name the same one
- gates: float32 [16384, 2], P('tm'), may hold values from 0.25 to 1
- w_gate: bfloat16 [64, 1024, 4096], P('tm', None, 'mp'), may hold values from -0.1875 to 0.1875
- w_up: bfloat16 [64, 1024, 4096], P('tm', None, 'mp'), may hold values from -0.1875 to 0.1875
- w_down: bfloat16 [64, 4096, 1024], P('tm', 'mp'), may hold values from -0.09375 to 0.09375
Outputs:
- layer_out: bfloat16 [16384, 1024], P('tm', 'mp')
Inputs may be any that keep to these rules, and one draw needn't show every extreme that they name: `segment_edges`: row 0 holds the first frame of each frame's segment and row 1 its last. Segments are runs of 1 to 64 frames; every multiple of 64 starts a segment, and some segment has exactly 64 frames. `expert_ids`: each frame names 2 different experts. Among the 512 frames of one index of tm no expert is named more than 32 times; in some of these groups one expert is named exactly 32 times.
All inputs are finite; a program needn't handle non-finite values.
Results may differ from a plain program's by a relative error of at most 0.006.
Values may be sent and summed in bfloat16 or wider, within the bound.
A program may use at most 128 MiB of HBM per device.

v0:
```python
import jax
import jax.numpy as jnp
from jax import lax
from jax.sharding import PartitionSpec as P

HEADS = 16
TOP = 2
LEFT = 256


EPS = 1e-06


def from_behind(x, axis, by):
    size = lax.axis_size(axis)
    pairs = [(i, i + by) for i in range(size) if 0 <= i + by < size]
    return lax.ppermute(x, axis, pairs)


def per_device(
    frames_in,
    queries,
    keys,
    values,
    segment_edges,
    out_proj,
    expert_ids,
    gates,
    w_gate,
    w_up,
    w_down,
):
    frames = frames_in.shape[0]
    model = frames_in.shape[1]
    columns = queries.shape[1]
    n_model = lax.axis_size("mp")
    n_time = lax.axis_size("tm")
    head_width = model // HEADS
    local_heads = columns // head_width
    scale = head_width ** (-0.5)
    reach = min(LEFT, frames)
    tail_rows = jnp.stack([keys[frames - reach :], values[frames - reach :]], 0)
    earlier = from_behind(tail_rows, "tm", 1)
    all_keys = jnp.concatenate([earlier[0], keys], 0)
    all_values = jnp.concatenate([earlier[1], values], 0)
    block = min(frames, 512)
    offset = lax.axis_index("tm") * frames
    query_rows = queries.reshape(block, local_heads, head_width)
    key_rows = all_keys.reshape(LEFT + block, local_heads, head_width)
    value_rows = all_values.reshape(LEFT + block, local_heads, head_width)
    places = offset - LEFT + 0 + jnp.arange(LEFT + block, dtype=jnp.int32)
    lower = jnp.maximum(segment_edges[0, 0:block] - LEFT, 0)
    upper = segment_edges[1, 0:block]
    visible = (places[None, :] >= lower[:, None]) & (places[None, :] <= upper[:, None])
    scores = (
        jnp.einsum("qhd,khd->hqk", query_rows, key_rows, preferred_element_type=jnp.float32) * scale
    )
    scores = jnp.where(visible[None], scores, -jnp.inf)
    highest = jnp.max(scores, -1, keepdims=True)
    expos = jnp.exp(scores - highest)
    weights = (expos / jnp.sum(expos, -1, keepdims=True)).astype(jnp.bfloat16)
    mixed = jnp.einsum("hqk,khd->qhd", weights, value_rows, preferred_element_type=jnp.float32)
    pieces = mixed.astype(jnp.bfloat16).reshape(block, columns)
    partial_attn = jnp.dot(pieces, out_proj, preferred_element_type=jnp.float32)
    share_width = model // n_model
    column_start = lax.axis_index("mp") * share_width
    summed = lax.psum(partial_attn, "mp")
    full_state = (frames_in.astype(jnp.float32) + summed).astype(jnp.bfloat16)
    full_state = lax.optimization_barrier(full_state)
    state = full_state.astype(jnp.float32)
    normed = (state * lax.rsqrt(jnp.mean(state * state, 1, keepdims=True) + EPS)).astype(
        jnp.bfloat16
    )
    residual = lax.dynamic_slice_in_dim(state, column_start, share_width, 1)
    experts_all = w_gate.shape[0] * n_time
    local_experts = w_gate.shape[0]
    capacity = 4 * frames // experts_all
    chosen = expert_ids.reshape(-1)
    onehot = (chosen[:, None] == jnp.arange(experts_all, dtype=jnp.int32)[None, :]).astype(
        jnp.int32
    )
    ranks = jnp.cumsum(onehot, 0) - onehot
    slots = jnp.sum(ranks * onehot, 1)
    targets = chosen * capacity + slots
    owners = jnp.arange(chosen.shape[0], dtype=jnp.int32) // TOP
    table = jnp.full((experts_all * capacity,), frames, jnp.int32).at[targets].set(owners)
    padded = jnp.concatenate([normed, jnp.zeros((1, model), jnp.bfloat16)], 0)
    outgoing = padded[table].reshape(n_time, local_experts, capacity, model)
    rows_in = lax.all_to_all(outgoing, "tm", split_axis=0, concat_axis=0, tiled=True)
    gate_act = jnp.einsum("sekd,edf->sekf", rows_in, w_gate, preferred_element_type=jnp.float32)
    up_act = jnp.einsum("sekd,edf->sekf", rows_in, w_up, preferred_element_type=jnp.float32)
    activity = (jax.nn.silu(gate_act) * up_act).astype(jnp.bfloat16)
    partial_out = jnp.einsum("sekf,efd->sekd", activity, w_down, preferred_element_type=jnp.float32)
    answer = lax.all_to_all(partial_out, "tm", split_axis=0, concat_axis=0, tiled=True)
    flat_back = answer.reshape(experts_all * capacity, answer.shape[3])
    picked = flat_back[targets].reshape(frames, TOP, answer.shape[3])
    mixture = jnp.sum(gates[:, :, None] * picked, 1)
    expert_sum = lax.psum_scatter(mixture, "mp", scatter_dimension=1, tiled=True)
    return (residual + expert_sum).astype(jnp.bfloat16)


def solution(mesh):
    return jax.shard_map(
        per_device,
        mesh=mesh,
        in_specs=(
            P("tm", None),
            P("tm", "mp"),
            P("tm", "mp"),
            P("tm", "mp"),
            P(None, "tm"),
            P("mp", None),
            P("tm", None),
            P("tm", None),
            P("tm", None, "mp"),
            P("tm", None, "mp"),
            P("tm", "mp", None),
        ),
        out_specs=P("tm", "mp"),
        check_vma=False,
    )
```

profile of v0, /device:TPU:32, one launch (start us, length us, event | category | flops | bytes accessed | tf_op | source)
XLA Modules:
  0.0 533.0 jit_solution(15622415219792034406)
XLA Ops:
  6.5 1.0 slice_bitcast_fusion
  7.6 3.8 collective-permute-start
  11.4 1.0 copy.36
  12.4 1.0 copy.34
  13.5 0.8 copy.41
  14.3 0.2 eq.29
  14.5 0.2 eq.25
  14.7 0.8 add_maximum_fusion
  15.4 1.0 copy.37
  16.5 18.0 %reduce-window.6 = s32[64,8,128]{2,1,0:T(8,128)S(1)} reduce-window(s32[64,8,128]{2,1,0:T(8,128)S(1)} %fusion.30, s32[]{:T(128)} %constant.25.clone.1), window={size=1x1x128 pad=0_0x0_0x127_0}, to_apply=%region_4.5 | reduce-window | flops 8323072 | bytes 524292 | tf_op jit(solution)/shard_map/reduce-window
  34.5 0.1 slice.38
  34.6 0.1 copy.43
  34.8 0.1 copy.44
  34.9 0.4 compare_and_fusion
  35.3 0.1 copy.35
  35.4 0.1 copy.33
  35.5 3.0 fusion.50
  38.5 2.3 fusion.24
  40.9 1.8 fusion.51
  42.7 0.0 all-reduce.3.cloned.1.call-update
  42.7 0.1 copy.40
  42.9 0.2 mul.71
  43.1 0.1 broadcast_add_fusion
  43.2 0.1 fusion.29
  43.3 4.3 scatter_custom_fusion
  47.6 67.7 %all-reduce.3.cloned.1.call-done = f32[512,1024]{1,0:T(8,128)} async-done(((f32[512,1024]{1,0:T(8,128)}), f32[512,1024]{1,0:T(8,128)}) %all-reduce.3.cloned.1.call-update) | async-done | bytes 2097168 | tf_op jit(solution)/shard_map/psum | solution.py:67
  115.3 2.2 add_convert_fusion
  117.5 0.3 multiply_reduce_fusion.1
  117.8 0.7 copy-done.2
  118.5 0.2 multiply_convert_fusion
  118.8 0.1 concatenate.25
  118.8 9.7 %gather_fusion = bf16[2048,1024]{1,0:T(8,128)(2,1)} fusion(bf16[513,1024]{1,0:T(8,128)(2,1)S(1)} %concatenate.25, s32[2048]{0:T(1024)S(1)} %fusion.35), kind=kCustom, calls=%fused_computation | custom fusion | bytes 8396800 | tf_op jit(solution)/shard_map/gather | solution.py:88
  128.5 104.4 %all_to_all.10 = bf16[32,2,32,1024]{3,2,1,0:T(8,128)(2,1)S(1)} all-to-all(bf16[32,2,32,1024]{3,2,1,0:T(8,128)(2,1)} %bitcast.88), channel_id=1, replica_groups=mesh['tm'=32,'mp'=8] {'tm'}, dimensions={0} | all-to-all | bytes 8388608 | tf_op jit(solution)/shard_map/all_to_all | solution.py:89
  232.9 2.0 copy-done.4
  234.9 4.3 fusion.5
  239.2 9.5 %convolution_bitcast_fusion = f32[32,2,32,1024]{3,2,0,1:T(8,128)} fusion(f32[2,32,32,512]{3,2,1,0:T(8,128)} %fusion.5, bf16[32,2,32,1024]{3,2,1,0:T(8,128)(2,1)} %copy-done.4, bf16[2,512,1024]{2,1,0:T(8,128)(2,1)S(1)} %copy-done, bf16[2,1024,512]{2,1,0:T(8,128)(2,1)} %param.19), kind=kOutput, calls=%fused_computation.16 | convolution fusion | flops 4301258752 | bytes 20971520 | tf_op jit(solution)/shard_map/sekf,efd->sekd/dot_general | solution.py:93
  248.7 8.3 %copy.47 = f32[32,2,32,1024]{3,2,1,0:T(8,128)} copy(f32[32,2,32,1024]{3,2,0,1:T(8,128)} %convolution_bitcast_fusion) | data formatting | bytes 16777216 | tf_op jit(solution)/shard_map/sekf,efd->sekd/transpose | solution.py:93
  257.0 5.2 all-to-all-start.1
  262.2 0.2 reduce-scatter.2.cloned.1.call-start
  262.4 0.1 copy.39
  262.6 182.4 %all-to-all-done.1 = f32[32,2,32,1024]{3,2,1,0:T(8,128)} async-done(((f32[32,2,32,1024]{3,2,1,0:T(8,128)}), f32[32,2,32,1024]{3,2,1,0:T(8,128)}, u32[]{:S(2)}, u32[]{:S(2)}) %all-to-all-start.1) | async-done | bytes 8388640 | tf_op jit(solution)/shard_map/all_to_all | solution.py:94
  445.0 9.8 %gather_fusion.1 = f32[1024,1024]{1,0:T(8,128)} fusion(f32[2048,1024]{1,0:T(8,128)} %bitcast.26, s32[1024]{0:T(1024)S(1)} %broadcast_clamp_fusion), kind=kCustom, calls=%fused_computation.1 | custom fusion | bytes 8392704 | tf_op jit(solution)/shard_map/gather | solution.py:96
  454.8 5.8 %reshape.155 = f32[512,2,1024]{2,1,0:T(2,128)} reshape(f32[1024,1024]{1,0:T(8,128)} %gather_fusion.1) | data formatting | bytes 8388608 | tf_op jit(solution)/shard_map/reshape | solution.py:96
  460.6 9.0 %multiply_reduce_fusion = f32[512,1024]{1,0:T(8,128)} fusion(f32[512,2,1024]{2,1,0:T(2,128)} %reshape.155, f32[512,2]{1,0:T(8,128)S(1)} %copy.39), kind=kLoop, calls=%fused_computation.11 | loop fusion | flops 1572864 | bytes 6295552 | tf_op jit(solution)/shard_map/reduce_sum | solution.py:97
  469.6 0.0 reduce-scatter.2.cloned.1.call-update
  469.6 1.6 convert_element_type.39
  471.2 53.2 %reduce-scatter.2.cloned.1.call-done = f32[512,128]{1,0:T(8,128)} async-done(((f32[512,1024]{1,0:T(8,128)}), f32[512,128]{1,0:T(8,128)}) %reduce-scatter.2.cloned.1.call-update) | async-done | bytes 262160 | tf_op jit(solution)/shard_map/reduce_scatter | solution.py:98
  524.5 1.7 add_convert_fusion.1
  (30 shorter events, 0.2 us)
Async XLA Ops:
  6.5 232.7 %copy-start = (bf16[2,512,1024]{2,1,0:T(8,128)(2,1)S(1)}, bf16[2,512,1024]{2,1,0:T(8,128)(2,1)}, u32[]{:S(2)}) copy-start(bf16[2,512,1024]{2,1,0:T(8,128)(2,1)} %param.21) | copy-start | bytes 6291460
  6.5 108.8 %all-reduce.3.cloned.1.call-start = ((), (), s32[]{:S(2)}) async-start(), calls=%async_computation.3 | async-start | bytes 4194304 | tf_op jit(solution)/shard_map/psum | solution.py:67
  7.6 27.7 %collective-permute-start = (bf16[2,256,128]{2,1,0:T(8,128)(2,1)S(1)}, bf16[2,256,128]{2,1,0:T(8,128)(2,1)S(1)}, u32[]{:S(2)}, u32[]{:S(2)}) collective-permute-start(bf16[2,256,128]{2,1,0:T(8,128)(2,1)S(1)} %pad_maximum_fusion.1), channel_id=1, source_target_pairs={{0,8},{8,16},{16,24},{24,32},{32,40},{40,48},{48,56},{56,64},{64,7... | collective-permute-start | bytes 393224 | tf_op jit(solution)/shard_map/ppermute | solution.py:17
  38.5 2.4 copy-start.5
  40.9 1.8 copy-start.6
  117.5 1.0 copy-start.2
  128.5 106.4 %copy-start.8 = (bf16[2,1024,512]{2,1,0:T(8,128)(2,1)S(1)}, bf16[2,1024,512]{2,1,0:T(8,128)(2,1)}, u32[]{:S(2)}) copy-start(bf16[2,1024,512]{2,1,0:T(8,128)(2,1)} %param.20) | copy-start | bytes 6291460
  232.9 2.0 copy-start.4
  257.0 5.4 %copy-start.7 = (f32[512,2]{0,1:T(2,128)S(1)}, f32[512,2]{0,1:T(2,128)}, u32[]{:S(2)}) copy-start(f32[512,2]{0,1:T(2,128)} %param.18) | copy-start | bytes 12292
  257.0 188.0 %all-to-all-start.1 = ((f32[32,2,32,1024]{3,2,1,0:T(8,128)}), f32[32,2,32,1024]{3,2,1,0:T(8,128)}, u32[]{:S(2)}, u32[]{:S(2)}) async-start(f32[32,2,32,1024]{3,2,1,0:T(8,128)} %copy.47), calls=%async_computation.1 | async-start | bytes 16777216 | tf_op jit(solution)/shard_map/all_to_all | solution.py:94
  262.2 262.3 %reduce-scatter.2.cloned.1.call-start = ((), (), s32[]{:S(2)}) async-start(), calls=%async_computation.4 | async-start | bytes 2359296 | tf_op jit(solution)/shard_map/reduce_scatter | solution.py:98
  460.6 9.0 %copy-start.3 = (bf16[512,1024]{1,0:T(8,128)(2,1)S(1)}, bf16[512,1024]{1,0:T(8,128)(2,1)}, u32[]{:S(2)}) copy-start(bf16[512,1024]{1,0:T(8,128)(2,1)} %copy-done.2) | copy-start | bytes 3145732
  460.6 65.6 %copy-start.1 = (bf16[2,512,1024]{2,1,0:T(8,128)(2,1)S(1)}, bf16[2,512,1024]{2,1,0:T(8,128)(2,1)}, u32[]{:S(2)}) copy-start(bf16[2,512,1024]{2,1,0:T(8,128)(2,1)} %param.21) | copy-start | bytes 6291460
Sparse Core Ops, SparseCore 0:
  42.8 72.4 all-reduce.2
  469.7 54.6 reduce-scatter.1
where the time goes:
time: 534 us; the launch traced here: 533 us
  waiting for transfers between devices  303 us (57%)
  blocking collectives  104 us (19%)
  local copies, waits for them, and re-layouts  46.9 us (9%)
  other arithmetic  34.5 us (6%)
  matrix products  20.9 us (4%)
  between operations  13.7 us (3%)
  starting transfers between devices  9.26 us (2%)
    all_to_all x1, waiting for transfers between devices, per_device(): lax.all_to_all(partial_out, 'tm', split_axis=0, concat_axis=0, tiled=True)  182 us
    all_to_all x1, blocking collectives, per_device(): lax.all_to_all(outgoing, 'tm', split_axis=0, concat_axis=0, tiled=True)  104 us
    psum x1, waiting for transfers between devices, per_device(): summed = lax.psum(partial_attn, 'mp')  67.7 us
    reduce_scatter x1, waiting for transfers between devices, per_device(): lax.psum_scatter(mixture, 'mp', scatter_dimension=1, tiled=True)  53.2 us
    another operation x3, other arithmetic  18.2 us
  transfers between devices with their start and end apart: 4, of which 3 were waited for; matrix products, arithmetic and copies ran while one was open for 6% of the time, Pallas kernels for 0%

commit v1 on v0

v1 whole, which is shorter than its diff:
```python
import functools

import jax
import jax.numpy as jnp
from jax import lax
from jax.experimental import pallas as pl
from jax.experimental.pallas import tpu as pltpu
from jax.sharding import PartitionSpec as P

HEADS = 16
LEFT = 256
EPS = 1e-06
NX = 4
NY = 4
QB = 128
MESH = pl.DeviceIdType.MESH
NEG = -1e30
BF = jnp.bfloat16
F32 = jnp.float32


def kernel(
    n_tm,
    cap,
    edges_ref,
    ids_ref,
    gates_ref,
    q_ref,
    k_hbm,
    v_hbm,
    f_hbm,
    wo_hbm,
    wg_hbm,
    wu_hbm,
    wd_hbm,
    out_ref,
    kbuf,
    vbuf,
    fbuf,
    wo,
    wg,
    wu,
    wd,
    ctx,
    hid,
    onehot,
    comb_hi,
    comb_lo,
    sbuf,
    xbuf,
    abuf,
    pown,
    psend,
    precv,
    q2,
    r2,
    q1,
    r1,
    hsend,
    rbuf,
    acc,
    loc_sem,
    halo_s,
    halo_r,
    wo_s,
    wo_r,
    c_s,
    c_r,
    d_s,
    d_r,
    e_s,
    e_r,
    g_s,
    g_r,
    h_s,
    h_r,
):
    t = lax.axis_index("tm")
    m = lax.axis_index("mp")
    nz = n_tm // NY
    y, z = t // nz, t % nz
    x, c = m // 2, m % 2
    x_r, x_l, x_o = (x + 1) % NX, (x + NX - 1) % NX, (x + 2) % NX
    m_r, m_l, m_o, m_s = x_r * 2 + c, x_l * 2 + c, x_o * 2 + c, x * 2 + 1 - c
    frames = q_ref.shape[0]
    n_exp = 2 * n_tm
    rc = nz * cap
    nxt, prv = (t + 1) % n_tm, (t + n_tm - 1) % n_tm

    def col(i):
        return pl.ds(pl.multiple_of(i * 128, 128), 128)

    def remote(src, dst, ss, rs, **dev):
        return pltpu.make_async_remote_copy(
            src_ref=src, dst_ref=dst, send_sem=ss, recv_sem=rs, device_id=dev, device_id_type=MESH
        )

    barrier = pltpu.get_barrier_semaphore()

    @pl.loop(1, n_tm)
    def _(i):
        pl.semaphore_signal(barrier, inc=1, device_id={"tm": (t + i) % n_tm}, device_id_type=MESH)

    @pl.loop(1, 2 * NX)
    def _(i):
        pl.semaphore_signal(barrier, inc=1, device_id={"mp": (m + i) % (2 * NX)}, device_id_type=MESH)

    own_k = pltpu.make_async_copy(k_hbm, kbuf.at[pl.ds(LEFT, frames)], loc_sem.at[0])
    own_v = pltpu.make_async_copy(v_hbm, vbuf.at[pl.ds(LEFT, frames)], loc_sem.at[1])
    own_f = pltpu.make_async_copy(f_hbm.at[:, col(m)], fbuf, loc_sem.at[2])
    own_o = pltpu.make_async_copy(
        wo_hbm.at[:, col(m)], wo.at[pl.ds(pl.multiple_of(m * 128, 128), 128)], loc_sem.at[3]
    )
    own_g = pltpu.make_async_copy(wg_hbm, wg, loc_sem.at[4])
    own_u = pltpu.make_async_copy(wu_hbm, wu, loc_sem.at[5])
    own_d = pltpu.make_async_copy(wd_hbm, wd, loc_sem.at[6])
    for copy in (own_k, own_v, own_f, own_o, own_g, own_u, own_d):
        copy.start()

    pl.semaphore_wait(barrier, n_tm - 1 + 2 * NX - 1)

    halo_k = remote(
        k_hbm.at[pl.ds(frames - LEFT, LEFT)], kbuf.at[pl.ds(0, LEFT)], halo_s.at[0], halo_r.at[0], tm=nxt
    )
    halo_v = remote(
        v_hbm.at[pl.ds(frames - LEFT, LEFT)], vbuf.at[pl.ds(0, LEFT)], halo_s.at[1], halo_r.at[1], tm=nxt
    )
    halo_k.start()
    halo_v.start()

    def wo_copy(i):
        peer = (m + i) % (2 * NX)
        return remote(
            wo_hbm.at[:, col(peer)],
            wo.at[pl.ds(pl.multiple_of(m * 128, 128), 128)],
            wo_s.at[i],
            wo_r.at[i],
            mp=peer,
        )

    @pl.loop(1, 2 * NX)
    def _(i):
        wo_copy(i).start()

    scale = (wo_hbm.shape[1] // HEADS) ** (-0.5)
    head = wo_hbm.shape[1] // HEADS
    lane = lax.broadcasted_iota(jnp.int32, (QB, 128), 1)
    win = LEFT + QB

    def attend(b):
        rows = pl.ds(pl.multiple_of(b * QB, QB), QB)
        keys = pl.ds(pl.multiple_of(b * QB, QB), win)
        q = q_ref[rows, :].astype(F32) * scale
        q_both = jnp.concatenate(
            [jnp.where(lane < head, q, 0.0), jnp.where(lane >= head, q, 0.0)], 0
        ).astype(BF)
        s = lax.dot_general(
            kbuf[keys, :], q_both, (((1,), (1,)), ((), ())), preferred_element_type=F32
        )
        lower = jnp.maximum(edges_ref[0:1, rows] - LEFT, 0)
        upper = edges_ref[1:2, rows]
        lower = jnp.concatenate([lower, lower], 1)
        upper = jnp.concatenate([upper, upper], 1)
        place = lax.broadcasted_iota(jnp.int32, (win, 2 * QB), 0) + (t * frames - LEFT + b * QB)
        s = jnp.where((place >= lower) & (place <= upper), s, NEG)
        p = jnp.exp(s - jnp.max(s, 0, keepdims=True))
        total = jnp.sum(p, 0, keepdims=True)
        v_t = vbuf[keys, :].astype(F32).T.astype(BF)
        o = jnp.dot(v_t, p.astype(BF), preferred_element_type=F32) / total
        both = jnp.concatenate([o[:head, :QB], o[head:, QB:]], 0)
        ctx[rows, col(m)] = both.T.astype(BF)

    half = frames // 2

    def c_rows(r):
        return pl.ds(pl.multiple_of(r * half, half), half)

    def c_half(r, h):
        return pl.ds(pl.multiple_of(r * half + h * (half // 2), half // 2), half // 2)

    def cx(r, k, rows, blk, dev):
        ref = ctx.at[rows, col(blk)]
        return remote(ref, ref, c_s.at[r, k], c_r.at[r, k], mp=dev)

    def c1(r):
        cx(r, 0, c_rows(r), m, m_r).start()
        cx(r, 1, c_rows(r), m, m_l).start()
        cx(r, 4, c_rows(r), m, m_s).start()

    def c2(r):
        cx(r, 0, c_rows(r), m_l, m_r).wait_recv()
        cx(r, 2, c_half(r, 0), m_l, m_r).start()
        cx(r, 1, c_rows(r), m_r, m_l).wait_recv()
        cx(r, 3, c_half(r, 1), m_r, m_l).start()
        cx(r, 5, c_rows(r), m_l, m_s).start()
        cx(r, 6, c_rows(r), m_r, m_s).start()

    def other(i):
        return i + 1 - 2 * c

    def c3(r):
        cx(r, 2, c_half(r, 0), m_o, m_r).wait_recv()
        cx(r, 3, c_half(r, 1), m_o, m_l).wait_recv()
        cx(r, 7, c_rows(r), m_o, m_s).start()
        cx(r, 4, c_rows(r), other(m), m_s).wait_recv()
        cx(r, 5, c_rows(r), other(m_l), m_s).wait_recv()
        cx(r, 6, c_rows(r), other(m_r), m_s).wait_recv()
        cx(r, 7, c_rows(r), other(m_o), m_s).wait_recv()

    def c_sent(r):
        cx(r, 0, c_rows(r), m, m_r).wait_send()
        cx(r, 1, c_rows(r), m, m_l).wait_send()
        cx(r, 2, c_half(r, 0), m_l, m_r).wait_send()
        cx(r, 3, c_half(r, 1), m_r, m_l).wait_send()
        cx(r, 4, c_rows(r), m, m_s).wait_send()
        cx(r, 5, c_rows(r), m_l, m_s).wait_send()
        cx(r, 6, c_rows(r), m_r, m_s).wait_send()
        cx(r, 7, c_rows(r), m_o, m_s).wait_send()

    own_k.wait()
    own_v.wait()
    per_half = half // QB

    @pl.loop(per_half, 2 * per_half)
    def _(b):
        attend(b)

    c1(1)
    halo_k.wait_recv()
    halo_v.wait_recv()

    @pl.loop(0, per_half)
    def _(b):
        attend(b)

    c1(0)
    c2(1)

    id0, id1 = ids_ref[0:1, :], ids_ref[1:2, :]
    e_iota = lax.broadcasted_iota(jnp.int32, (n_exp, frames), 0)
    is0, is1 = e_iota == id0, e_iota == id1
    named = jnp.where(is0 | is1, 1.0, 0.0).astype(BF)
    before = jnp.where(
        lax.broadcasted_iota(jnp.int32, (frames, frames), 0)
        < lax.broadcasted_iota(jnp.int32, (frames, frames), 1),
        1.0,
        0.0,
    ).astype(BF)
    ranks = jnp.dot(named, before, preferred_element_type=F32)
    slot0 = jnp.sum(jnp.where(is0, ranks, 0.0), 0, keepdims=True).astype(jnp.int32)
    slot1 = jnp.sum(jnp.where(is1, ranks, 0.0), 0, keepdims=True).astype(jnp.int32)
    tgt0, tgt1 = id0 * cap + slot0, id1 * cap + slot1

    @pl.loop(0, n_exp * cap // 128)
    def _(i):
        rows = pl.ds(pl.multiple_of(i * 128, 128), 128)
        place = lax.broadcasted_iota(jnp.int32, (128, frames), 0) + i * 128
        onehot[rows, :] = jnp.where((place == tgt0) | (place == tgt1), 1.0, 0.0).astype(BF)

    c3(1)
    c2(0)

    @pl.loop(1, 2 * NX)
    def _(i):
        wo_copy(i).wait_recv()

    own_o.wait()
    own_f.wait()

    def hidden(r):
        rows = c_rows(r)
        hid[rows, :] = (
            fbuf[rows, :].astype(F32) + jnp.dot(ctx[rows, :], wo[...], preferred_element_type=F32)
        ).astype(BF)

    hidden(1)
    c3(0)
    hidden(0)

    def d_copy(ty, i):
        d = ty * nz + (z + i) % nz
        return remote(
            sbuf.at[d],
            xbuf.at[:, pl.ds(pl.multiple_of(t * cap, cap), cap), col(m)],
            d_s.at[d],
            d_r.at[t],
            tm=d,
        )

    def d_own():
        return pltpu.make_async_copy(
            sbuf.at[t],
            xbuf.at[:, pl.ds(pl.multiple_of(t * cap, cap), cap), col(m)],
            d_r.at[t],
        )

    def d_wait(src):
        return remote(
            sbuf.at[src],
            xbuf.at[:, pl.ds(pl.multiple_of(src * cap, cap), cap), col(m)],
            d_s.at[src],
            d_r.at[src],
            tm=src,
        )

    @pl.loop(0, NY)
    def _(j):
        ty = (y + NY - j) % NY
        rows = pl.ds(pl.multiple_of(ty * (2 * rc), 2 * rc), 2 * rc)
        sent = jnp.dot(onehot[rows, :], hid[...], preferred_element_type=F32)
        sbuf[pl.ds(ty * nz, nz)] = sent.astype(BF).reshape(nz, 2, cap, 128)

        @pl.loop(0, nz)
        def _(i):
            stays = (j == 0) & (i == 0)

            @pl.when(stays)
            def _():
                d_own().start()

            @pl.when(jnp.logical_not(stays))
            def _():
                d_copy(ty, i).start()

    g0, g1 = gates_ref[0:1, :], gates_ref[1:2, :]
    g0_hi, g1_hi = g0.astype(BF).astype(F32), g1.astype(BF).astype(F32)
    g0_lo, g1_lo = g0 - g0_hi, g1 - g1_hi

    @pl.loop(0, n_exp * cap // 128)
    def _(i):
        rows = pl.ds(pl.multiple_of(i * 128, 128), 128)
        place = lax.broadcasted_iota(jnp.int32, (128, frames), 0) + i * 128
        at0, at1 = place == tgt0, place == tgt1
        comb_hi[rows, :] = jnp.where(at0, g0_hi, jnp.where(at1, g1_hi, 0.0)).astype(BF)
        comb_lo[rows, :] = jnp.where(at0, g0_lo, jnp.where(at1, g1_lo, 0.0)).astype(BF)

    def src_y(j):
        return (y + j) % NY

    def e_rows(j):
        return pl.ds(pl.multiple_of(src_y(j) * rc, rc), rc)

    def ex(j, k, ref, dev):
        return remote(ref, ref, e_s.at[j, k], e_r.at[j, k], mp=dev)

    def e_blk(j, blk):
        return xbuf.at[:, e_rows(j), col(blk)]

    def e_half(j, h, blk):
        return xbuf.at[h, e_rows(j), col(blk)]

    def e1(j):
        @pl.loop(0, nz)
        def _(i):
            stays = (j == 0) & (i == 0)

            @pl.when(stays)
            def _():
                d_own().wait()

            @pl.when(jnp.logical_not(stays))
            def _():
                d_wait(src_y(j) * nz + (z + nz - i) % nz).wait_recv()

        ex(j, 0, e_blk(j, m), m_r).start()
        ex(j, 1, e_blk(j, m), m_l).start()
        ex(j, 4, e_blk(j, m), m_s).start()

    def e2(j):
        ex(j, 0, e_blk(j, m_l), m_r).wait_recv()
        ex(j, 2, e_half(j, 0, m_l), m_r).start()
        ex(j, 1, e_blk(j, m_r), m_l).wait_recv()
        ex(j, 3, e_half(j, 1, m_r), m_l).start()
        ex(j, 5, e_blk(j, m_l), m_s).start()
        ex(j, 6, e_blk(j, m_r), m_s).start()

    def e3(j):
        ex(j, 2, e_half(j, 0, m_o), m_r).wait_recv()
        ex(j, 3, e_half(j, 1, m_o), m_l).wait_recv()
        ex(j, 7, e_blk(j, m_o), m_s).start()

    def e4(j):
        ex(j, 4, e_blk(j, other(m)), m_s).wait_recv()
        ex(j, 5, e_blk(j, other(m_l)), m_s).wait_recv()
        ex(j, 6, e_blk(j, other(m_r)), m_s).wait_recv()
        ex(j, 7, e_blk(j, other(m_o)), m_s).wait_recv()

    def e_sent(j):
        ex(j, 0, e_blk(j, m), m_r).wait_send()
        ex(j, 1, e_blk(j, m), m_l).wait_send()
        ex(j, 2, e_half(j, 0, m_l), m_r).wait_send()
        ex(j, 3, e_half(j, 1, m_r), m_l).wait_send()
        ex(j, 4, e_blk(j, m), m_s).wait_send()
        ex(j, 5, e_blk(j, m_l), m_s).wait_send()
        ex(j, 6, e_blk(j, m_r), m_s).wait_send()
        ex(j, 7, e_blk(j, m_o), m_s).wait_send()

    def g_sib(j, e):
        return remote(psend.at[j, e], precv.at[j, e], g_s.at[j, e], g_r.at[j, e], mp=m_s)

    def g_far(j, h, dev):
        return remote(q2.at[j, h], r2.at[j, h], g_s.at[j, 2 + h], g_r.at[j, 2 + h], mp=dev)

    def g_near(j, h, dev):
        return remote(q1.at[j, h], r1.at[j, h], g_s.at[j, 4 + h], g_r.at[j, 4 + h], mp=dev)

    def experts(j):
        rows = e_rows(j)

        @pl.loop(0, 2)
        def _(e):
            v = xbuf[e, rows, :].astype(F32)
            inv = lax.rsqrt(jnp.mean(v * v, 1, keepdims=True) + EPS)
            normed = (v * inv).astype(BF)
            g = jnp.dot(normed, wg[e], preferred_element_type=F32)
            u = jnp.dot(normed, wu[e], preferred_element_type=F32)
            a = (g / (1.0 + jnp.exp(-g)) * u).astype(BF)
            abuf[...] = a
            w_far = jnp.concatenate([wd[e, :, col(i * 2 + 1 - c)] for i in range(NX)], 1)
            o_far = jnp.dot(abuf[...], w_far, preferred_element_type=F32).astype(BF)
            for i in range(NX):
                psend[j, e, i] = o_far[:, i * 128 : (i + 1) * 128]
            g_sib(j, e).start()
            w_own = jnp.concatenate([wd[e, :, col(i * 2 + c)] for i in range(NX)], 1)
            o_own = jnp.dot(abuf[...], w_own, preferred_element_type=F32)
            for i in range(NX):
                pown[j, e, i] = o_own[:, i * 128 : (i + 1) * 128]

    def both(j, e, blk):
        return pown[j, e, blk] + precv[j, e, blk].astype(F32)

    def g1(j):
        g_sib(j, 0).wait_recv()
        q2[j, 0] = both(j, 0, x_o).astype(BF)
        g_far(j, 0, m_r).start()
        g_sib(j, 1).wait_recv()
        q2[j, 1] = both(j, 1, x_o).astype(BF)
        g_far(j, 1, m_l).start()

    def g2(j):
        q1[j, 0, 1] = both(j, 1, x_r).astype(BF)
        q1[j, 1, 0] = both(j, 0, x_l).astype(BF)
        g_far(j, 0, m_r).wait_recv()
        q1[j, 0, 0] = (both(j, 0, x_r) + r2[j, 0].astype(F32)).astype(BF)
        g_near(j, 0, m_r).start()
        g_far(j, 1, m_l).wait_recv()
        q1[j, 1, 1] = (both(j, 1, x_l) + r2[j, 1].astype(F32)).astype(BF)
        g_near(j, 1, m_l).start()

    def h_copy(j, i):
        d = src_y(j) * nz + (z + nz - i) % nz
        return remote(
            hsend.at[j, :, pl.ds(pl.multiple_of((d % nz) * cap, cap), cap), :],
            rbuf.at[t],
            h_s.at[d],
            h_r.at[t],
            tm=d,
        )

    def h_own():
        return pltpu.make_async_copy(
            hsend.at[0, :, pl.ds(pl.multiple_of(z * cap, cap), cap), :], rbuf.at[t], h_r.at[t]
        )

    def h_wait(src):
        return remote(rbuf.at[src], rbuf.at[src], h_s.at[src], h_r.at[src], tm=src)

    def g3(j):
        g_near(j, 0, m_r).wait_recv()
        g_near(j, 1, m_l).wait_recv()
        for e in range(2):
            hsend[j, e] = (
                both(j, e, x) + r1[j, 0, e].astype(F32) + r1[j, 1, e].astype(F32)
            ).astype(BF)

        @pl.loop(0, nz)
        def _(i):
            stays = (j == 0) & (i == 0)

            @pl.when(stays)
            def _():
                h_own().start()

            @pl.when(jnp.logical_not(stays))
            def _():
                h_copy(j, i).start()

    def g_sent(j):
        for e in range(2):
            g_sib(j, e).wait_send()
        g_far(j, 0, m_r).wait_send()
        g_far(j, 1, m_l).wait_send()
        g_near(j, 0, m_r).wait_send()
        g_near(j, 1, m_l).wait_send()

    own_g.wait()
    own_u.wait()
    own_d.wait()

    def stage(k, f):
        @pl.when((k >= 0) & (k < NY))
        def _():
            f(k)

    @pl.loop(0, NY + 5)
    def _(tick):
        stage(tick - 1, e2)
        stage(tick, e1)
        stage(tick - 2, e3)
        stage(tick - 5, g3)
        stage(tick - 4, g2)
        stage(tick - 3, g1)
        stage(tick - 2, e4)
        stage(tick - 2, experts)

    acc[...] = jnp.zeros_like(acc)

    @pl.loop(0, NY)
    def _(j):
        oy = (y + NY - j) % NY

        @pl.loop(0, nz)
        def _(i):
            stays = (j == 0) & (i == 0)

            @pl.when(stays)
            def _():
                h_own().wait()

            @pl.when(jnp.logical_not(stays))
            def _():
                h_wait(oy * nz + (z + i) % nz).wait_recv()

        rows = pl.ds(pl.multiple_of(oy * (2 * rc), 2 * rc), 2 * rc)
        back = rbuf[pl.ds(oy * nz, nz)].reshape(2 * rc, 128)
        back_t = back.astype(F32).T.astype(BF)
        acc[...] += jnp.dot(back_t, comb_hi[rows, :], preferred_element_type=F32) + jnp.dot(
            back_t, comb_lo[rows, :], preferred_element_type=F32
        )

    out_ref[...] = (hid[...].astype(F32) + acc[...].T).astype(BF)

    halo_k.wait_send()
    halo_v.wait_send()

    @pl.loop(1, 2 * NX)
    def _(i):
        wo_copy(i).wait_send()

    @pl.loop(0, 2)
    def _(r):
        c_sent(r)

    @pl.loop(0, NY)
    def _(j):
        e_sent(j)
        g_sent(j)

        @pl.loop(0, nz)
        def _(i):
            stays = (j == 0) & (i == 0)

            @pl.when(jnp.logical_not(stays))
            def _():
                d_copy((y + NY - j) % NY, i).wait_send()
                h_copy(j, i).wait_send()


def per_device(
    frames_in,
    queries,
    keys,
    values,
    segment_edges,
    out_proj,
    expert_ids,
    gates,
    w_gate,
    w_up,
    w_down,
):
    frames = frames_in.shape[0]
    n_tm = lax.axis_size("tm")
    model = frames_in.shape[1]
    inner = w_gate.shape[2]
    n_exp = w_gate.shape[0] * n_tm
    cap = 4 * frames // n_exp
    rc = n_tm // NY * cap
    slots = n_exp * cap
    vmem = pl.BlockSpec(memory_space=pltpu.VMEM)
    anyw = pl.BlockSpec(memory_space=pl.ANY)
    dma = pltpu.SemaphoreType.DMA
    return pl.pallas_call(
        functools.partial(kernel, n_tm, cap),
        out_shape=jax.ShapeDtypeStruct((frames, 128), BF),
        in_specs=[vmem] * 4 + [anyw] * 7,
        out_specs=vmem,
        scratch_shapes=[
            pltpu.VMEM((LEFT + frames, 128), BF),
            pltpu.VMEM((LEFT + frames, 128), BF),
            pltpu.VMEM((frames, 128), BF),
            pltpu.VMEM((model, 128), BF),
            pltpu.VMEM(w_gate.shape, BF),
            pltpu.VMEM(w_up.shape, BF),
            pltpu.VMEM(w_down.shape, BF),
            pltpu.VMEM((frames, model), BF),
            pltpu.VMEM((frames, 128), BF),
            pltpu.VMEM((slots, frames), BF),
            pltpu.VMEM((slots, frames), BF),
            pltpu.VMEM((slots, frames), BF),
            pltpu.VMEM((n_tm, 2, cap, 128), BF),
            pltpu.VMEM((2, n_tm * cap, model), BF),
            pltpu.VMEM((rc, inner), BF),
            pltpu.VMEM((NY, 2, NX, rc, 128), F32),
            pltpu.VMEM((NY, 2, NX, rc, 128), BF),
            pltpu.VMEM((NY, 2, NX, rc, 128), BF),
            pltpu.VMEM((NY, 2, rc, 128), BF),
            pltpu.VMEM((NY, 2, rc, 128), BF),
            pltpu.VMEM((NY, 2, 2, rc, 128), BF),
            pltpu.VMEM((NY, 2, 2, rc, 128), BF),
            pltpu.VMEM((NY, 2, rc, 128), BF),
            pltpu.VMEM((n_tm, 2, cap, 128), BF),
            pltpu.VMEM((128, frames), F32),
            dma((7,)),
            dma((2,)),
            dma((2,)),
            dma((2 * NX,)),
            dma((2 * NX,)),
            dma((2, 8)),
            dma((2, 8)),
            dma((n_tm,)),
            dma((n_tm,)),
            dma((NY, 8)),
            dma((NY, 8)),
            dma((NY, 6)),
            dma((NY, 6)),
            dma((n_tm,)),
            dma((n_tm,)),
        ],
        compiler_params=pltpu.CompilerParams(
            collective_id=0, has_side_effects=True, vmem_limit_bytes=56 * 1024 * 1024
        ),
        name="layer",
    )(
        segment_edges,
        expert_ids.T,
        gates.T,
        queries,
        keys,
        values,
        frames_in,
        out_proj,
        w_gate,
        w_up,
        w_down,
    )


def solution(mesh):
    return jax.shard_map(
        per_device,
        mesh=mesh,
        in_specs=(
            P("tm", None),
            P("tm", "mp"),
            P("tm", "mp"),
            P("tm", "mp"),
            P(None, "tm"),
            P("mp", None),
            P("tm", None),
            P("tm", None),
            P("tm", None, "mp"),
            P("tm", None, "mp"),
            P("tm", "mp", None),
        ),
        out_specs=P("tm", "mp"),
        check_vma=False,
    )
```

time: 534 us -> 92.6 us (0.17)
  waiting for transfers between devices: 303 us -> 0 us
  blocking collectives: 104 us -> 0 us
  Pallas kernels: 0 us -> 90.8 us
  local copies, waits for them, and re-layouts: 46.9 us -> 1.57 us
  other arithmetic: 34.5 us -> 0 us
  matrix products: 20.9 us -> 0 us
  between operations: 13.7 us -> 0.01 us
  starting transfers between devices: 9.26 us -> 0 us
    all_to_all x1 -> x0, waiting for transfers between devices: 182 us -> none  [per_device(): lax.all_to_all(partial_out, 'tm', split_axis=0, concat_axis=0, tiled=True)]
    all_to_all x1 -> x0, blocking collectives: 104 us -> none  [per_device(): lax.all_to_all(outgoing, 'tm', split_axis=0, concat_axis=0, tiled=True)]
    pallas_call x0 -> x1, Pallas kernels: none -> 90.8 us  [per_device(): pl.pallas_call(functools.partial(kernel, n_tm, cap), out_shape=jax.ShapeD...]
    psum x1 -> x0, waiting for transfers between devices: 67.7 us -> none  [per_device(): summed = lax.psum(partial_attn, 'mp')]
    reduce_scatter x1 -> x0, waiting for transfers between devices: 53.2 us -> none  [per_device(): lax.psum_scatter(mixture, 'mp', scatter_dimension=1, tiled=True)]
    gather x2 -> x0, local copies, waits for them, and re-layouts: 19.5 us -> none  [the longest x1 9.82 us: per_device(): picked = flat_back[targets].reshape(frames, TOP, answer.shape[3])]
    another operation x4 -> x0, other arithmetic: 18.2 us -> none
    dot_general x4 -> x0, matrix products: 17.9 us -> none  [the longest x1 9.52 us: per_device(): jnp.einsum('sekf,efd->sekd', activity, w_down, preferred_element_type=jnp...]
  transfers between devices with their start and end apart: 4 -> 0, of which waited for: 3 -> 0; matrix products, arithmetic and copies ran while one was open for 6% -> 0% of each run, Pallas kernels for 0% -> 0%
where the time goes in v1:
time: 92.6 us; the launch traced here: 92.3 us
  Pallas kernels  90.8 us (98%)
  local copies, waits for them, and re-layouts  1.57 us (2%)
    pallas_call x1, Pallas kernels, per_device(): pl.pallas_call(functools.partial(kernel, n_tm, cap), out_shape=jax.ShapeD...  90.8 us

profile of v1, /device:TPU:32, one launch (start us, length us, event | category | flops | bytes accessed | tf_op | source)
XLA Modules:
  0.0 92.3 jit_solution(2676692398238498622)
XLA Ops:
  0.0 90.8 %layer.1 = bf16[512,128]{1,0:T(8,128)(2,1)} custom-call(s32[2,512]{1,0:T(2,128)} %edges_ref.1, s32[2,512]{1,0:T(2,128)} %bitcast.2, f32[2,512]{1,0:T(2,128)} %bitcast.3, bf16[512,128]{1,0:T(8,128)(2,1)} %q_ref.1, bf16[512,128]{1,0:T(8,128)(2,1)} %k_hbm.1, bf16[512,128]{1,0:T(8,128)(2,1)} %v_hbm.1, bf16[512,1024]{1,0:T(8,128)(2,1)} %f_hbm.1, ...), custom_call_target="tpu_custom_call" | custom-call | tf_op jit(solution)/shard_map/layer/pallas_call | solution.py:593
  90.8 1.6 %copy.13 = bf16[512,128]{1,0:T(8,128)(2,1)} copy(bf16[512,128]{1,0:T(8,128)(2,1)} %layer.1) | data formatting | bytes 262144

commit v2 on v1

v2 whole, which is shorter than its diff:
```python
import functools

import jax
import jax.numpy as jnp
from jax import lax
from jax.experimental import pallas as pl
from jax.experimental.pallas import tpu as pltpu
from jax.sharding import PartitionSpec as P

HEADS = 16
LEFT = 256
EPS = 1e-06
NX = 4
NY = 4
QB = 128
PARTS = 4
AHEAD = (0, 2, 4, 5, 7, 9, 11)
ORDER = (0, 1, 2, 4, 5, 6, 3)
MESH = pl.DeviceIdType.MESH
NEG = -1e30
BF = jnp.bfloat16
F32 = jnp.float32


def relative_order(nz, parts):
    cells = sorted(
        ((dy, dz) for dy in range(NY) for dz in range(nz)),
        key=lambda o: min(o[0], NY - o[0]) + min(o[1], nz - o[1]),
    )
    size = len(cells) // parts
    groups = [cells[i * size : (i + 1) * size] for i in range(parts)]
    return sum(groups[::2] + groups[1::2][::-1], [])


def kernel(
    n_tm,
    cap,
    parts,
    edges_ref,
    ids_ref,
    gates_ref,
    q_ref,
    k_hbm,
    v_hbm,
    f_hbm,
    wo_hbm,
    wg_hbm,
    wu_hbm,
    wd_hbm,
    out_ref,
    kbuf,
    vbuf,
    fbuf,
    wo,
    wg,
    wu,
    wd,
    ctx,
    hid,
    onehot,
    comb_hi,
    comb_lo,
    sbuf,
    xbuf,
    abuf,
    pown,
    psend,
    precv,
    q2,
    r2,
    q1,
    r1,
    hsend,
    rbuf,
    acc,
    loc_sem,
    halo_s,
    halo_r,
    wo_s,
    wo_r,
    c_s,
    c_r,
    d_s,
    d_r,
    e_s,
    e_r,
    g_s,
    g_r,
    h_s,
    h_r,
    know,
):
    t = lax.axis_index("tm")
    m = lax.axis_index("mp")
    nz = n_tm // NY
    y, z = t // nz, t % nz
    x, c = m // 2, m % 2
    x_r, x_l, x_o = (x + 1) % NX, (x + NX - 1) % NX, (x + 2) % NX
    m_r, m_l, m_o, m_s = x_r * 2 + c, x_l * 2 + c, x_o * 2 + c, x * 2 + 1 - c
    frames = q_ref.shape[0]
    n_exp = 2 * n_tm
    per = n_tm // parts
    rc = per * cap
    chunks = 2 * parts
    offsets = relative_order(nz, parts)
    nxt, prv = (t + 1) % n_tm, (t + n_tm - 1) % n_tm

    def col(i):
        return pl.ds(pl.multiple_of(i * 128, 128), 128)

    def remote(src, dst, ss, rs, **dev):
        return pltpu.make_async_remote_copy(
            src_ref=src, dst_ref=dst, send_sem=ss, recv_sem=rs, device_id=dev, device_id_type=MESH
        )

    barrier = pltpu.get_barrier_semaphore()

    def tell(sem, dy, dz):
        pl.semaphore_signal(
            sem, inc=1, device_id={"tm": (y + dy) % NY * nz + (z + dz) % nz}, device_id_type=MESH
        )

    for dy in range(1, NY):
        tell(barrier, dy, 0)
    if nz > 1:
        tell(barrier, 0, 1)
        tell(barrier, 0, nz - 1)
    for peer in (nxt, prv):
        pl.semaphore_signal(barrier, inc=1, device_id={"tm": peer}, device_id_type=MESH)

    @pl.loop(1, 2 * NX)
    def _(i):
        pl.semaphore_signal(barrier, inc=1, device_id={"mp": (m + i) % (2 * NX)}, device_id_type=MESH)

    own_k = pltpu.make_async_copy(k_hbm, kbuf.at[pl.ds(LEFT, frames)], loc_sem.at[0])
    own_v = pltpu.make_async_copy(v_hbm, vbuf.at[pl.ds(LEFT, frames)], loc_sem.at[1])
    own_f = pltpu.make_async_copy(f_hbm.at[:, col(m)], fbuf, loc_sem.at[2])
    own_o = pltpu.make_async_copy(
        wo_hbm.at[:, col(m)], wo.at[pl.ds(pl.multiple_of(m * 128, 128), 128)], loc_sem.at[3]
    )
    own_g = pltpu.make_async_copy(wg_hbm, wg, loc_sem.at[4])
    own_u = pltpu.make_async_copy(wu_hbm, wu, loc_sem.at[5])
    own_d = pltpu.make_async_copy(wd_hbm, wd, loc_sem.at[6])
    for copy in (own_k, own_v, own_f, own_o, own_g, own_u, own_d):
        copy.start()

    halo_k = remote(
        k_hbm.at[pl.ds(frames - LEFT, LEFT)], kbuf.at[pl.ds(0, LEFT)], halo_s.at[0], halo_r.at[0], tm=nxt
    )
    halo_v = remote(
        v_hbm.at[pl.ds(frames - LEFT, LEFT)], vbuf.at[pl.ds(0, LEFT)], halo_s.at[1], halo_r.at[1], tm=nxt
    )

    def wo_copy(i):
        peer = (m + i) % (2 * NX)
        return remote(
            wo_hbm.at[:, col(peer)],
            wo.at[pl.ds(pl.multiple_of(m * 128, 128), 128)],
            wo_s.at[i],
            wo_r.at[i],
            mp=peer,
        )

    scale = (wo_hbm.shape[1] // HEADS) ** (-0.5)
    head = wo_hbm.shape[1] // HEADS
    lane = lax.broadcasted_iota(jnp.int32, (QB, 128), 1)
    win = LEFT + QB

    def attend(b):
        rows = pl.ds(pl.multiple_of(b * QB, QB), QB)
        keys = pl.ds(pl.multiple_of(b * QB, QB), win)
        q = q_ref[rows, :].astype(F32) * scale
        q_both = jnp.concatenate(
            [jnp.where(lane < head, q, 0.0), jnp.where(lane >= head, q, 0.0)], 0
        ).astype(BF)
        s = lax.dot_general(
            kbuf[keys, :], q_both, (((1,), (1,)), ((), ())), preferred_element_type=F32
        )
        lower = jnp.maximum(edges_ref[0:1, rows] - LEFT, 0)
        upper = edges_ref[1:2, rows]
        lower = jnp.concatenate([lower, lower], 1)
        upper = jnp.concatenate([upper, upper], 1)
        place = lax.broadcasted_iota(jnp.int32, (win, 2 * QB), 0) + (t * frames - LEFT + b * QB)
        s = jnp.where((place >= lower) & (place <= upper), s, NEG)
        p = jnp.exp(s - jnp.max(s, 0, keepdims=True))
        total = jnp.sum(p, 0, keepdims=True)
        v_t = vbuf[keys, :].astype(F32).T.astype(BF)
        o = jnp.dot(v_t, p.astype(BF), preferred_element_type=F32) / total
        both = jnp.concatenate([o[:head, :QB], o[head:, QB:]], 0)
        ctx[rows, col(m)] = both.T.astype(BF)

    half = frames // 2

    def c_rows(r):
        return pl.ds(pl.multiple_of(r * half, half), half)

    def cx(r, k, rows, blk, dev):
        ref = ctx.at[rows, col(blk)]
        return remote(ref, ref, c_s.at[r, k], c_r.at[r, k], mp=dev)

    def c1(r):
        cx(r, 0, c_rows(r), m, m_r).start()
        cx(r, 1, c_rows(r), m, m_l).start()
        cx(r, 2, c_rows(r), m, m_o).start()
        cx(r, 3, c_rows(r), m, m_s).start()

    def other(i):
        return i + 1 - 2 * c

    def c2(r):
        cx(r, 0, c_rows(r), m_l, m_r).wait_recv()
        cx(r, 4, c_rows(r), m_l, m_s).start()
        cx(r, 1, c_rows(r), m_r, m_l).wait_recv()
        cx(r, 5, c_rows(r), m_r, m_s).start()
        cx(r, 2, c_rows(r), m_o, m_o).wait_recv()
        cx(r, 6, c_rows(r), m_o, m_s).start()

    def c3(r):
        cx(r, 3, c_rows(r), other(m), m_s).wait_recv()
        cx(r, 4, c_rows(r), other(m_l), m_s).wait_recv()
        cx(r, 5, c_rows(r), other(m_r), m_s).wait_recv()
        cx(r, 6, c_rows(r), other(m_o), m_s).wait_recv()

    def c_sent(r):
        cx(r, 0, c_rows(r), m, m_r).wait_send()
        cx(r, 1, c_rows(r), m, m_l).wait_send()
        cx(r, 2, c_rows(r), m, m_o).wait_send()
        cx(r, 3, c_rows(r), m, m_s).wait_send()
        cx(r, 4, c_rows(r), m_l, m_s).wait_send()
        cx(r, 5, c_rows(r), m_r, m_s).wait_send()
        cx(r, 6, c_rows(r), m_o, m_s).wait_send()

    own_k.wait()
    own_v.wait()
    per_half = half // QB

    @pl.loop(per_half, 2 * per_half)
    def _(b):
        attend(b)

    pl.semaphore_wait(barrier, NY - 1 + 2 * (nz > 1) + 2 + 2 * NX - 1)
    halo_k.start()
    halo_v.start()
    c1(1)

    @pl.loop(1, 2 * NX)
    def _(i):
        wo_copy(i).start()

    if nz > 1:
        tell(know.at[0], 0, 1)
        tell(know.at[0], 0, nz - 1)

    id0, id1 = ids_ref[0:1, :], ids_ref[1:2, :]
    e_iota = lax.broadcasted_iota(jnp.int32, (n_exp, frames), 0)
    is0, is1 = e_iota == id0, e_iota == id1
    named = jnp.where(is0 | is1, 1.0, 0.0).astype(BF)
    before = jnp.where(
        lax.broadcasted_iota(jnp.int32, (frames, frames), 0)
        < lax.broadcasted_iota(jnp.int32, (frames, frames), 1),
        1.0,
        0.0,
    ).astype(BF)
    ranks = jnp.dot(named, before, preferred_element_type=F32)
    slot0 = jnp.sum(jnp.where(is0, ranks, 0.0), 0, keepdims=True).astype(jnp.int32)
    slot1 = jnp.sum(jnp.where(is1, ranks, 0.0), 0, keepdims=True).astype(jnp.int32)
    owner = lax.broadcasted_iota(jnp.int32, (n_exp, frames), 0)
    first = jnp.zeros((n_exp, frames), jnp.int32)
    for p, (dy, dz) in enumerate(offsets):
        d = (y + NY - dy) % NY * nz + (z + nz - dz) % nz
        first = jnp.where((owner == 2 * d) | (owner == 2 * d + 1), (2 * p - 2 * d) * cap, first)
    first = first + owner * cap
    tgt0 = slot0 + jnp.sum(jnp.where(is0, first, 0), 0, keepdims=True)
    tgt1 = slot1 + jnp.sum(jnp.where(is1, first, 0), 0, keepdims=True)

    @pl.loop(0, n_exp * cap // 128)
    def _(i):
        rows = pl.ds(pl.multiple_of(i * 128, 128), 128)
        place = lax.broadcasted_iota(jnp.int32, (128, frames), 0) + i * 128
        onehot[rows, :] = jnp.where((place == tgt0) | (place == tgt1), 1.0, 0.0).astype(BF)

    if nz > 1:
        pl.semaphore_wait(know.at[0], 2)
        tell(know.at[1], 0, 2 % nz)
        tell(know.at[1], 0, nz - 2)
    c2(1)
    halo_k.wait_recv()
    halo_v.wait_recv()

    @pl.loop(0, per_half)
    def _(b):
        attend(b)

    c1(0)
    c3(1)
    if nz > 1:
        pl.semaphore_wait(know.at[1], 2)
    for dy in range(1, NY):
        tell(know.at[2], dy, 0)

    g0, g1 = gates_ref[0:1, :], gates_ref[1:2, :]
    g0_hi, g1_hi = g0.astype(BF).astype(F32), g1.astype(BF).astype(F32)
    g0_lo, g1_lo = g0 - g0_hi, g1 - g1_hi

    @pl.loop(0, n_exp * cap // 128)
    def _(i):
        rows = pl.ds(pl.multiple_of(i * 128, 128), 128)
        place = lax.broadcasted_iota(jnp.int32, (128, frames), 0) + i * 128
        at0, at1 = place == tgt0, place == tgt1
        comb_hi[rows, :] = jnp.where(at0, g0_hi, jnp.where(at1, g1_hi, 0.0)).astype(BF)
        comb_lo[rows, :] = jnp.where(at0, g0_lo, jnp.where(at1, g1_lo, 0.0)).astype(BF)

    @pl.loop(1, 2 * NX)
    def _(i):
        wo_copy(i).wait_recv()

    own_o.wait()
    own_f.wait()

    def hidden(r):
        rows = c_rows(r)
        hid[rows, :] = (
            fbuf[rows, :].astype(F32) + jnp.dot(ctx[rows, :], wo[...], preferred_element_type=F32)
        ).astype(BF)

    hidden(1)
    c2(0)
    c3(0)
    hidden(0)
    pl.semaphore_wait(know.at[2], NY - 1)

    def tm_at(p, sign):
        dy, dz = offsets[p]
        return (y + NY + sign * dy) % NY * nz + (z + nz + sign * dz) % nz

    def x_rows(p):
        return pl.ds(p * cap, cap)

    def d_copy(p):
        if p == 0:
            return pltpu.make_async_copy(sbuf.at[p], xbuf.at[:, x_rows(p), col(m)], d_r.at[p])
        return remote(
            sbuf.at[p], xbuf.at[:, x_rows(p), col(m)], d_s.at[p], d_r.at[p], tm=tm_at(p, -1)
        )

    def d_wait(p):
        if p == 0:
            d_copy(p).wait()
        else:
            d_copy(p).wait_recv()

    sent_rows = n_tm * 2 * cap // 4
    for i in range(4):
        sent = jnp.dot(
            onehot[i * sent_rows : (i + 1) * sent_rows, :], hid[...], preferred_element_type=F32
        )
        sbuf[i * n_tm // 4 : (i + 1) * n_tm // 4] = sent.astype(BF).reshape(n_tm // 4, 2, cap, 128)
        for p in range(i * n_tm // 4, (i + 1) * n_tm // 4):
            d_copy(p).start()

    def e_rows(j):
        return pl.ds(pl.multiple_of(j // 2 * rc, rc), rc)

    def ex(j, k, ref, dev):
        return remote(ref, ref, e_s.at[j, k], e_r.at[j, k], mp=dev)

    def e_blk(j, blk):
        return xbuf.at[j % 2, e_rows(j), col(blk)]

    def e_half(j, h, blk):
        rows = pl.ds(pl.multiple_of(j // 2 * rc + h * (rc // 2), rc // 2), rc // 2)
        return xbuf.at[j % 2, rows, col(blk)]

    def e1(j):
        for k in range(parts):

            @pl.when(j == 2 * k)
            def _(k=k):
                for p in range(k * per, (k + 1) * per):
                    d_wait(p)

        ex(j, 0, e_blk(j, m), m_r).start()
        ex(j, 1, e_blk(j, m), m_l).start()
        ex(j, 4, e_blk(j, m), m_s).start()

    def e2(j):
        ex(j, 0, e_blk(j, m_l), m_r).wait_recv()
        ex(j, 2, e_half(j, 0, m_l), m_r).start()
        ex(j, 1, e_blk(j, m_r), m_l).wait_recv()
        ex(j, 3, e_half(j, 1, m_r), m_l).start()
        ex(j, 5, e_blk(j, m_l), m_s).start()
        ex(j, 6, e_blk(j, m_r), m_s).start()

    def e3(j):
        ex(j, 2, e_half(j, 0, m_o), m_r).wait_recv()
        ex(j, 3, e_half(j, 1, m_o), m_l).wait_recv()
        ex(j, 7, e_blk(j, m_o), m_s).start()

    def e4(j):
        ex(j, 4, e_blk(j, other(m)), m_s).wait_recv()
        ex(j, 5, e_blk(j, other(m_l)), m_s).wait_recv()
        ex(j, 6, e_blk(j, other(m_r)), m_s).wait_recv()
        ex(j, 7, e_blk(j, other(m_o)), m_s).wait_recv()

    def e_sent(j):
        ex(j, 0, e_blk(j, m), m_r).wait_send()
        ex(j, 1, e_blk(j, m), m_l).wait_send()
        ex(j, 2, e_half(j, 0, m_l), m_r).wait_send()
        ex(j, 3, e_half(j, 1, m_r), m_l).wait_send()
        ex(j, 4, e_blk(j, m), m_s).wait_send()
        ex(j, 5, e_blk(j, m_l), m_s).wait_send()
        ex(j, 6, e_blk(j, m_r), m_s).wait_send()
        ex(j, 7, e_blk(j, m_o), m_s).wait_send()

    def g_sib(j):
        return remote(psend.at[j], precv.at[j], g_s.at[j, 0], g_r.at[j, 0], mp=m_s)

    def g_far(j, h, dev):
        return remote(q2.at[j, h], r2.at[j, h], g_s.at[j, 1 + h], g_r.at[j, 1 + h], mp=dev)

    def g_near(j, h, dev):
        return remote(q1.at[j, h], r1.at[j, h], g_s.at[j, 3 + h], g_r.at[j, 3 + h], mp=dev)

    def experts(j):
        e4(j)
        e = j % 2
        v = xbuf[e, e_rows(j), :].astype(F32)
        inv = lax.rsqrt(jnp.mean(v * v, 1, keepdims=True) + EPS)
        normed = (v * inv).astype(BF)
        g = jnp.dot(normed, wg[e], preferred_element_type=F32)
        u = jnp.dot(normed, wu[e], preferred_element_type=F32)
        abuf[...] = (g / (1.0 + jnp.exp(-g)) * u).astype(BF)
        w_far = jnp.concatenate([wd[e, :, col(i * 2 + 1 - c)] for i in range(NX)], 1)
        o_far = jnp.dot(abuf[...], w_far, preferred_element_type=F32).astype(BF)
        for i in range(NX):
            psend[j, i] = o_far[:, i * 128 : (i + 1) * 128]
        g_sib(j).start()
        w_own = jnp.concatenate([wd[e, :, col(i * 2 + c)] for i in range(NX)], 1)
        o_own = jnp.dot(abuf[...], w_own, preferred_element_type=F32)
        for i in range(NX):
            pown[j, i] = o_own[:, i * 128 : (i + 1) * 128]

    halves = (slice(0, rc // 2), slice(rc // 2, rc))

    def both(j, blk, rows=slice(None)):
        return pown[j, blk, rows] + precv[j, blk, rows].astype(F32)

    def g1(j):
        g_sib(j).wait_recv()
        q2[j, 0] = both(j, x_o, halves[0]).astype(BF)
        g_far(j, 0, m_r).start()
        q2[j, 1] = both(j, x_o, halves[1]).astype(BF)
        g_far(j, 1, m_l).start()
        q1[j, 0, halves[1]] = both(j, x_r, halves[1]).astype(BF)
        q1[j, 1, halves[0]] = both(j, x_l, halves[0]).astype(BF)

    def g2(j):
        g_far(j, 0, m_r).wait_recv()
        q1[j, 0, halves[0]] = (both(j, x_r, halves[0]) + r2[j, 0].astype(F32)).astype(BF)
        g_near(j, 0, m_r).start()
        g_far(j, 1, m_l).wait_recv()
        q1[j, 1, halves[1]] = (both(j, x_l, halves[1]) + r2[j, 1].astype(F32)).astype(BF)
        g_near(j, 1, m_l).start()

    def h_copy(p):
        k, i = divmod(p, per)
        src = hsend.at[k, :, pl.ds(i * cap, cap), :]
        if p == 0:
            return pltpu.make_async_copy(src, rbuf.at[p], h_r.at[p])
        return remote(src, rbuf.at[p], h_s.at[p], h_r.at[p], tm=tm_at(p, 1))

    def g3(j):
        g_near(j, 0, m_r).wait_recv()
        g_near(j, 1, m_l).wait_recv()
        hsend[j // 2, j % 2] = (
            both(j, x) + r1[j, 0].astype(F32) + r1[j, 1].astype(F32)
        ).astype(BF)

        for k in range(parts):

            @pl.when(j == 2 * k + 1)
            def _(k=k):
                for p in range(k * per, (k + 1) * per):
                    h_copy(p).start()

    def g_sent(j):
        g_sib(j).wait_send()
        g_far(j, 0, m_r).wait_send()
        g_far(j, 1, m_l).wait_send()
        g_near(j, 0, m_r).wait_send()
        g_near(j, 1, m_l).wait_send()

    own_g.wait()
    own_u.wait()
    own_d.wait()

    def stage(k, f):
        @pl.when((k >= 0) & (k < chunks))
        def _():
            f(k)

    @pl.loop(0, chunks + AHEAD[-1])
    def _(tick):
        for k in ORDER:
            stage(tick - AHEAD[k], (e1, e2, e3, experts, g1, g2, g3)[k])

    acc[...] = jnp.zeros_like(acc)
    for k in range(parts):
        mine = range(k * per, (k + 1) * per)
        for p in mine:
            if p == 0:
                h_copy(p).wait()
            else:
                h_copy(p).wait_recv()
        rows = slice(2 * rc * k, 2 * rc * (k + 1))
        back = rbuf[mine.start : mine.stop].reshape(2 * rc, 128)
        back_t = back.astype(F32).T.astype(BF)
        acc[...] += jnp.dot(back_t, comb_hi[rows, :], preferred_element_type=F32) + jnp.dot(
            back_t, comb_lo[rows, :], preferred_element_type=F32
        )

    out_ref[...] = (hid[...].astype(F32) + acc[...].T).astype(BF)

    halo_k.wait_send()
    halo_v.wait_send()

    @pl.loop(1, 2 * NX)
    def _(i):
        wo_copy(i).wait_send()

    @pl.loop(0, 2)
    def _(r):
        c_sent(r)

    @pl.loop(0, chunks)
    def _(j):
        e_sent(j)
        g_sent(j)

    for p in range(1, n_tm):
        d_copy(p).wait_send()
        h_copy(p).wait_send()


def per_device(
    frames_in,
    queries,
    keys,
    values,
    segment_edges,
    out_proj,
    expert_ids,
    gates,
    w_gate,
    w_up,
    w_down,
):
    frames = frames_in.shape[0]
    n_tm = lax.axis_size("tm")
    model = frames_in.shape[1]
    inner = w_gate.shape[2]
    n_exp = w_gate.shape[0] * n_tm
    cap = 4 * frames // n_exp
    parts = PARTS
    chunks = 2 * parts
    rc = n_tm // parts * cap
    slots = n_exp * cap
    vmem = pl.BlockSpec(memory_space=pltpu.VMEM)
    anyw = pl.BlockSpec(memory_space=pl.ANY)
    dma = pltpu.SemaphoreType.DMA
    return pl.pallas_call(
        functools.partial(kernel, n_tm, cap, parts),
        out_shape=jax.ShapeDtypeStruct((frames, 128), BF),
        in_specs=[vmem] * 4 + [anyw] * 7,
        out_specs=vmem,
        scratch_shapes=[
            pltpu.VMEM((LEFT + frames, 128), BF),
            pltpu.VMEM((LEFT + frames, 128), BF),
            pltpu.VMEM((frames, 128), BF),
            pltpu.VMEM((model, 128), BF),
            pltpu.VMEM(w_gate.shape, BF),
            pltpu.VMEM(w_up.shape, BF),
            pltpu.VMEM(w_down.shape, BF),
            pltpu.VMEM((frames, model), BF),
            pltpu.VMEM((frames, 128), BF),
            pltpu.VMEM((slots, frames), BF),
            pltpu.VMEM((slots, frames), BF),
            pltpu.VMEM((slots, frames), BF),
            pltpu.VMEM((n_tm, 2, cap, 128), BF),
            pltpu.VMEM((2, n_tm * cap, model), BF),
            pltpu.VMEM((rc, inner), BF),
            pltpu.VMEM((chunks, NX, rc, 128), F32),
            pltpu.VMEM((chunks, NX, rc, 128), BF),
            pltpu.VMEM((chunks, NX, rc, 128), BF),
            pltpu.VMEM((chunks, 2, rc // 2, 128), BF),
            pltpu.VMEM((chunks, 2, rc // 2, 128), BF),
            pltpu.VMEM((chunks, 2, rc, 128), BF),
            pltpu.VMEM((chunks, 2, rc, 128), BF),
            pltpu.VMEM((parts, 2, rc, 128), BF),
            pltpu.VMEM((n_tm, 2, cap, 128), BF),
            pltpu.VMEM((128, frames), F32),
            dma((7,)),
            dma((2,)),
            dma((2,)),
            dma((2 * NX,)),
            dma((2 * NX,)),
            dma((2, 8)),
            dma((2, 8)),
            dma((n_tm,)),
            dma((n_tm,)),
            dma((chunks, 8)),
            dma((chunks, 8)),
            dma((chunks, 5)),
            dma((chunks, 5)),
            dma((n_tm,)),
            dma((n_tm,)),
            pltpu.SemaphoreType.REGULAR((3,)),
        ],
        compiler_params=pltpu.CompilerParams(
            collective_id=0, has_side_effects=True, vmem_limit_bytes=56 * 1024 * 1024
        ),
        name="layer",
    )(
        segment_edges,
        expert_ids.T,
        gates.T,
        queries,
        keys,
        values,
        frames_in,
        out_proj,
        w_gate,
        w_up,
        w_down,
    )


def solution(mesh):
    return jax.shard_map(
        per_device,
        mesh=mesh,
        in_specs=(
            P("tm", None),
            P("tm", "mp"),
            P("tm", "mp"),
            P("tm", "mp"),
            P(None, "tm"),
            P("mp", None),
            P("tm", None),
            P("tm", None),
            P("tm", None, "mp"),
            P("tm", None, "mp"),
            P("tm", "mp", None),
        ),
        out_specs=P("tm", "mp"),
        check_vma=False,
    )
```

time: 92.6 us -> 81.9 us (0.88)
  Pallas kernels: 90.8 us -> 79.7 us
    pallas_call x1, Pallas kernels: 90.8 us -> 79.7 us  [per_device(): pl.pallas_call(functools.partial(kernel, n_tm, cap, parts), out_shape=jax...]
where the time goes in v2:
time: 81.9 us; the launch traced here: 81.3 us
  Pallas kernels  79.7 us (97%)
  local copies, waits for them, and re-layouts  1.57 us (2%)
    pallas_call x1, Pallas kernels, per_device(): pl.pallas_call(functools.partial(kernel, n_tm, cap, parts), out_shape=jax...  79.7 us

profile of v2, /device:TPU:32, one launch (start us, length us, event | category | flops | bytes accessed | tf_op | source)
XLA Modules:
  0.0 81.3 jit_solution(14961300600858258803)
XLA Ops:
  0.0 79.7 %layer.1 = bf16[512,128]{1,0:T(8,128)(2,1)} custom-call(s32[2,512]{1,0:T(2,128)} %edges_ref.1, s32[2,512]{1,0:T(2,128)} %bitcast.2, f32[2,512]{1,0:T(2,128)} %bitcast.3, bf16[512,128]{1,0:T(8,128)(2,1)} %q_ref.1, bf16[512,128]{1,0:T(8,128)(2,1)} %k_hbm.1, bf16[512,128]{1,0:T(8,128)(2,1)} %v_hbm.1, bf16[512,1024]{1,0:T(8,128)(2,1)} %f_hbm.1, ...), custom_call_target="tpu_custom_call" | custom-call | tf_op jit(solution)/shard_map/layer/pallas_call | solution.py:571
  79.7 1.6 %copy.13 = bf16[512,128]{1,0:T(8,128)(2,1)} copy(bf16[512,128]{1,0:T(8,128)(2,1)} %layer.1) | data formatting | bytes 262144

commit v3 on v2

--- a/solution.py
+++ b/solution.py
@@ -15,7 +15,7 @@
 QB = 128
 PARTS = 4
 AHEAD = (0, 2, 4, 5, 7, 9, 11)
-ORDER = (0, 1, 2, 4, 5, 6, 3)
+ORDER = (0, 6, 5, 4, 1, 2, 3)
 MESH = pl.DeviceIdType.MESH
 NEG = -1e30
 BF = jnp.bfloat16
@@ -187,7 +187,7 @@
         v_t = vbuf[keys, :].astype(F32).T.astype(BF)
         o = jnp.dot(v_t, p.astype(BF), preferred_element_type=F32) / total
         both = jnp.concatenate([o[:head, :QB], o[head:, QB:]], 0)
-        ctx[rows, col(m)] = both.T.astype(BF)
+        ctx[m, rows] = both.T.astype(BF)
 
     half = frames // 2
 
@@ -195,7 +195,7 @@
         return pl.ds(pl.multiple_of(r * half, half), half)
 
     def cx(r, k, rows, blk, dev):
-        ref = ctx.at[rows, col(blk)]
+        ref = ctx.at[blk, rows]
         return remote(ref, ref, c_s.at[r, k], c_r.at[r, k], mp=dev)
 
     def c1(r):
@@ -319,8 +319,9 @@
 
     def hidden(r):
         rows = c_rows(r)
+        mixed = jnp.concatenate([ctx[b, rows] for b in range(2 * NX)], 1)
         hid[rows, :] = (
-            fbuf[rows, :].astype(F32) + jnp.dot(ctx[rows, :], wo[...], preferred_element_type=F32)
+            fbuf[rows, :].astype(F32) + jnp.dot(mixed, wo[...], preferred_element_type=F32)
         ).astype(BF)
 
     hidden(1)
@@ -329,6 +330,9 @@
     hidden(0)
     pl.semaphore_wait(know.at[2], NY - 1)
 
+    def spot(i):
+        return i % 2 * NX + i // 2 % 2 * 2 + i // 4
+
     def tm_at(p, sign):
         dy, dz = offsets[p]
         return (y + NY + sign * dy) % NY * nz + (z + nz + sign * dz) % nz
@@ -338,9 +342,9 @@
 
     def d_copy(p):
         if p == 0:
-            return pltpu.make_async_copy(sbuf.at[p], xbuf.at[:, x_rows(p), col(m)], d_r.at[p])
+            return pltpu.make_async_copy(sbuf.at[p], xbuf.at[spot(m), :, x_rows(p)], d_r.at[p])
         return remote(
-            sbuf.at[p], xbuf.at[:, x_rows(p), col(m)], d_s.at[p], d_r.at[p], tm=tm_at(p, -1)
+            sbuf.at[p], xbuf.at[spot(m), :, x_rows(p)], d_s.at[p], d_r.at[p], tm=tm_at(p, -1)
         )
 
     def d_wait(p):
@@ -365,11 +369,16 @@
         return remote(ref, ref, e_s.at[j, k], e_r.at[j, k], mp=dev)
 
     def e_blk(j, blk):
-        return xbuf.at[j % 2, e_rows(j), col(blk)]
+        return xbuf.at[spot(blk), j % 2, e_rows(j)]
 
     def e_half(j, h, blk):
         rows = pl.ds(pl.multiple_of(j // 2 * rc + h * (rc // 2), rc // 2), rc // 2)
-        return xbuf.at[j % 2, rows, col(blk)]
+        return xbuf.at[spot(blk), j % 2, rows]
+
+    def e_pair(j, core, odd):
+        return xbuf.at[pl.ds(core * NX + odd * 2, 2), j % 2, e_rows(j)]
+
+    near, same = (x + 1) % 2, x % 2
 
     def e1(j):
         for k in range(parts):
@@ -381,36 +390,30 @@
 
         ex(j, 0, e_blk(j, m), m_r).start()
         ex(j, 1, e_blk(j, m), m_l).start()
-        ex(j, 4, e_blk(j, m), m_s).start()
 
     def e2(j):
         ex(j, 0, e_blk(j, m_l), m_r).wait_recv()
         ex(j, 2, e_half(j, 0, m_l), m_r).start()
         ex(j, 1, e_blk(j, m_r), m_l).wait_recv()
         ex(j, 3, e_half(j, 1, m_r), m_l).start()
-        ex(j, 5, e_blk(j, m_l), m_s).start()
-        ex(j, 6, e_blk(j, m_r), m_s).start()
+        ex(j, 4, e_pair(j, c, near), m_s).start()
 
     def e3(j):
         ex(j, 2, e_half(j, 0, m_o), m_r).wait_recv()
         ex(j, 3, e_half(j, 1, m_o), m_l).wait_recv()
-        ex(j, 7, e_blk(j, m_o), m_s).start()
+        ex(j, 5, e_pair(j, c, same), m_s).start()
 
     def e4(j):
-        ex(j, 4, e_blk(j, other(m)), m_s).wait_recv()
-        ex(j, 5, e_blk(j, other(m_l)), m_s).wait_recv()
-        ex(j, 6, e_blk(j, other(m_r)), m_s).wait_recv()
-        ex(j, 7, e_blk(j, other(m_o)), m_s).wait_recv()
+        ex(j, 4, e_pair(j, 1 - c, near), m_s).wait_recv()
+        ex(j, 5, e_pair(j, 1 - c, same), m_s).wait_recv()
 
     def e_sent(j):
         ex(j, 0, e_blk(j, m), m_r).wait_send()
         ex(j, 1, e_blk(j, m), m_l).wait_send()
         ex(j, 2, e_half(j, 0, m_l), m_r).wait_send()
         ex(j, 3, e_half(j, 1, m_r), m_l).wait_send()
-        ex(j, 4, e_blk(j, m), m_s).wait_send()
-        ex(j, 5, e_blk(j, m_l), m_s).wait_send()
-        ex(j, 6, e_blk(j, m_r), m_s).wait_send()
-        ex(j, 7, e_blk(j, m_o), m_s).wait_send()
+        ex(j, 4, e_pair(j, c, near), m_s).wait_send()
+        ex(j, 5, e_pair(j, c, same), m_s).wait_send()
 
     def g_sib(j):
         return remote(psend.at[j], precv.at[j], g_s.at[j, 0], g_r.at[j, 0], mp=m_s)
@@ -424,7 +427,7 @@
     def experts(j):
         e4(j)
         e = j % 2
-        v = xbuf[e, e_rows(j), :].astype(F32)
+        v = jnp.concatenate([xbuf[spot(b), e, e_rows(j)] for b in range(2 * NX)], 1).astype(F32)
         inv = lax.rsqrt(jnp.mean(v * v, 1, keepdims=True) + EPS)
         normed = (v * inv).astype(BF)
         g = jnp.dot(normed, wg[e], preferred_element_type=F32)
@@ -504,8 +507,32 @@
         for k in ORDER:
             stage(tick - AHEAD[k], (e1, e2, e3, experts, g1, g2, g3)[k])
 
+    def sent():
+        halo_k.wait_send()
+        halo_v.wait_send()
+
+        @pl.loop(1, 2 * NX)
+        def _(i):
+            wo_copy(i).wait_send()
+
+        @pl.loop(0, 2)
+        def _(r):
+            c_sent(r)
+
+        @pl.loop(0, chunks)
+        def _(j):
+            e_sent(j)
+            g_sent(j)
+
+        for p in range(1, n_tm):
+            d_copy(p).wait_send()
+        for p in range(1, (parts - 1) * per):
+            h_copy(p).wait_send()
+
     acc[...] = jnp.zeros_like(acc)
     for k in range(parts):
+        if k == parts - 1:
+            sent()
         mine = range(k * per, (k + 1) * per)
         for p in mine:
             if p == 0:
@@ -521,25 +548,9 @@
 
     out_ref[...] = (hid[...].astype(F32) + acc[...].T).astype(BF)
 
-    halo_k.wait_send()
-    halo_v.wait_send()
-
-    @pl.loop(1, 2 * NX)
-    def _(i):
-        wo_copy(i).wait_send()
-
-    @pl.loop(0, 2)
-    def _(r):
-        c_sent(r)
-
-    @pl.loop(0, chunks)
-    def _(j):
-        e_sent(j)
-        g_sent(j)
-
-    for p in range(1, n_tm):
-        d_copy(p).wait_send()
-        h_copy(p).wait_send()
+    for p in range((parts - 1) * per, n_tm):
+        if p > 0:
+            h_copy(p).wait_send()
 
 
 def per_device(
@@ -581,13 +592,13 @@
             pltpu.VMEM(w_gate.shape, BF),
             pltpu.VMEM(w_up.shape, BF),
             pltpu.VMEM(w_down.shape, BF),
-            pltpu.VMEM((frames, model), BF),
+            pltpu.VMEM((model // 128, frames, 128), BF),
             pltpu.VMEM((frames, 128), BF),
             pltpu.VMEM((slots, frames), BF),
             pltpu.VMEM((slots, frames), BF),
             pltpu.VMEM((slots, frames), BF),
             pltpu.VMEM((n_tm, 2, cap, 128), BF),
-            pltpu.VMEM((2, n_tm * cap, model), BF),
+            pltpu.VMEM((model // 128, 2, n_tm * cap, 128), BF),
             pltpu.VMEM((rc, inner), BF),
             pltpu.VMEM((chunks, NX, rc, 128), F32),
             pltpu.VMEM((chunks, NX, rc, 128), BF),
@@ -608,8 +619,8 @@
             dma((2, 8)),
             dma((n_tm,)),
             dma((n_tm,)),
-            dma((chunks, 8)),
-            dma((chunks, 8)),
+            dma((chunks, 6)),
+            dma((chunks, 6)),
             dma((chunks, 5)),
             dma((chunks, 5)),
             dma((n_tm,)),

time: 81.9 us -> 80.5 us (0.983)
  Pallas kernels: 79.7 us -> 78.6 us
    pallas_call x1, Pallas kernels: 79.7 us -> 78.6 us  [per_device(): pl.pallas_call(functools.partial(kernel, n_tm, cap, parts), out_shape=jax...]
where the time goes in v3:
time: 80.5 us; the launch traced here: 80.2 us
  Pallas kernels  78.6 us (98%)
  local copies, waits for them, and re-layouts  1.57 us (2%)
    pallas_call x1, Pallas kernels, per_device(): pl.pallas_call(functools.partial(kernel, n_tm, cap, parts), out_shape=jax...  78.6 us

profile of v3, /device:TPU:32, one launch (start us, length us, event | category | flops | bytes accessed | tf_op | source)
XLA Modules:
  0.0 80.2 jit_solution(14534166353978975633)
XLA Ops:
  0.0 78.6 %layer.1 = bf16[512,128]{1,0:T(8,128)(2,1)} custom-call(s32[2,512]{1,0:T(2,128)} %edges_ref.1, s32[2,512]{1,0:T(2,128)} %bitcast.2, f32[2,512]{1,0:T(2,128)} %bitcast.3, bf16[512,128]{1,0:T(8,128)(2,1)} %q_ref.1, bf16[512,128]{1,0:T(8,128)(2,1)} %k_hbm.1, bf16[512,128]{1,0:T(8,128)(2,1)} %v_hbm.1, bf16[512,1024]{1,0:T(8,128)(2,1)} %f_hbm.1, ...), custom_call_target="tpu_custom_call" | custom-call | tf_op jit(solution)/shard_map/layer/pallas_call | solution.py:582
  78.6 1.6 %copy.13 = bf16[512,128]{1,0:T(8,128)(2,1)} copy(bf16[512,128]{1,0:T(8,128)(2,1)} %layer.1) | data formatting | bytes 262144

commit v4 on v3

--- a/solution.py
+++ b/solution.py
@@ -230,6 +230,9 @@
         cx(r, 5, c_rows(r), m_r, m_s).wait_send()
         cx(r, 6, c_rows(r), m_o, m_s).wait_send()
 
+    pl.semaphore_wait(barrier, NY - 1 + 2 * (nz > 1) + 2 + 2 * NX - 1)
+    halo_k.start()
+    halo_v.start()
     own_k.wait()
     own_v.wait()
     per_half = half // QB
@@ -238,9 +241,6 @@
     def _(b):
         attend(b)
 
-    pl.semaphore_wait(barrier, NY - 1 + 2 * (nz > 1) + 2 + 2 * NX - 1)
-    halo_k.start()
-    halo_v.start()
     c1(1)
 
     @pl.loop(1, 2 * NX)

time: 80.5 us -> 82.4 us (1.024)
  Pallas kernels: 78.6 us -> 80.8 us
    pallas_call x1, Pallas kernels: 78.6 us -> 80.8 us  [per_device(): pl.pallas_call(functools.partial(kernel, n_tm, cap, parts), out_shape=jax...]
where the time goes in v4:
time: 82.4 us; the launch traced here: 82.3 us
  Pallas kernels  80.8 us (98%)
  local copies, waits for them, and re-layouts  1.57 us (2%)
    pallas_call x1, Pallas kernels, per_device(): pl.pallas_call(functools.partial(kernel, n_tm, cap, parts), out_shape=jax...  80.8 us

profile of v4, /device:TPU:32, one launch (start us, length us, event | category | flops | bytes accessed | tf_op | source)
XLA Modules:
  0.0 82.3 jit_solution(9164446895826070598)
XLA Ops:
  0.0 80.8 %layer.1 = bf16[512,128]{1,0:T(8,128)(2,1)} custom-call(s32[2,512]{1,0:T(2,128)} %edges_ref.1, s32[2,512]{1,0:T(2,128)} %bitcast.2, f32[2,512]{1,0:T(2,128)} %bitcast.3, bf16[512,128]{1,0:T(8,128)(2,1)} %q_ref.1, bf16[512,128]{1,0:T(8,128)(2,1)} %k_hbm.1, bf16[512,128]{1,0:T(8,128)(2,1)} %v_hbm.1, bf16[512,1024]{1,0:T(8,128)(2,1)} %f_hbm.1, ...), custom_call_target="tpu_custom_call" | custom-call | tf_op jit(solution)/shard_map/layer/pallas_call | solution.py:582
  80.8 1.6 %copy.13 = bf16[512,128]{1,0:T(8,128)(2,1)} copy(bf16[512,128]{1,0:T(8,128)(2,1)} %layer.1) | data formatting | bytes 262144
